TPU v7x, 128 devices: a whole 4x4x4 slice. The times are simulated.
128 devices in a mesh: grp: 4 (over y), cand: 32 (over x, z, core).
Axes of the slice: x: 4, y: 4, z: 4, core: 2. Of those that a mesh axis runs over, the one named last changes fastest.
Arguments:
- node_emb: bfloat16 [32, 512, 512], P('cand'), may hold values from -6 to 6
- rel_emb: float32 [900, 512], P('grp'), may hold values from -6 to 6
- w_in: bfloat16 [512, 512], replicated, may hold values from -0.25 to 0.25
- w_self: bfloat16 [512, 512], replicated, may hold values from -1 to 1
- rel_score: float32 [900, 512], replicated, may hold values from -7 to 7
- mirror_blocks: int32 [4, 32, 32, 1], P('grp', 'cand'), may hold values from 0 to 3
- adj_values: bfloat16 [4, 32, 192, 128, 128], P('grp', 'cand'), may hold values from -0.0390625 to 0.0390625
- adj_source: int32 [4, 32, 192], P('grp', 'cand'), may hold values from 0 to 31
- adj_target: int32 [4, 32, 192], P('grp', 'cand'), may hold values from 0 to 3
- adj_relation: int32 [4, 32, 192], P('grp', 'cand'), may hold values from 0 to 224
- live_blocks: int32 [4, 32], P('grp', 'cand'), may hold values from 48 to 192, as said below
- query_head: int32 [1024], replicated, may hold values from 0 to 16383
- query_rel: int32 [1024], replicated, may hold values from 0 to 899
- allowed: int32 [1024, 8], replicated, may hold values from 0 to 127, as said below
- true_tail: int32 [1024], replicated, may hold values from 0 to 16383, as said below
Outputs:
- h_out: bfloat16 [32, 512, 512], P('cand', 'grp')
- loss: float32 [1024], replicated
- grad_h: float32 [32, 512, 512], P('cand', 'grp')
- grad_rel: float32 [900, 512], P('grp')
- grad_w_in: float32 [512, 512], replicated
- grad_w_self: float32 [512, 512], replicated
Inputs may be any that keep to these rules, and one draw needn't show every extreme that they name: `live_blocks`: blocks from this count on are padding; on some device all 192 blocks are live. `allowed`: ids of blocks of 128 concepts; a query may name a block twice. `true_tail`: lies in one of the query's allowed blocks.
All inputs are finite; a program needn't handle non-finite values.
Results may differ from a plain program's by a relative error of at most 0.011.
Values may be sent and summed in bfloat16 or wider, within the bound.
A program may use at most 128 MiB of HBM per device.

v0:
```python
import math
import jax
import jax.numpy as jnp
from jax import lax
from jax.sharding import PartitionSpec as P

NEG_FILL = -1e30
HIGH = lax.Precision.HIGHEST


def body(
    node_emb,
    rel_emb,
    w_in,
    w_self,
    rel_score,
    mirror_blocks,
    adj_values,
    adj_source,
    adj_target,
    adj_relation,
    live_blocks,
    query_head,
    query_rel,
    allowed,
    true_tail,
):
    cand_count = lax.axis_size("cand")
    grp_count = lax.axis_size("grp")
    grp_index = lax.axis_index("grp")
    cand_index = lax.axis_index("cand")
    nodes = node_emb[0]
    node_rows, feature_dim = nodes.shape
    block_rows = adj_values.shape[-1]
    tile_count = node_rows // block_rows
    share_rows = node_rows // grp_count
    wanted = mirror_blocks[0, 0]
    slot_count = wanted.shape[1]
    mirror_count = cand_count * slot_count
    requested = lax.all_to_all(wanted, "cand", split_axis=0, concat_axis=0, tiled=True)
    everything = lax.all_gather(node_emb, "cand", axis=0, tiled=True)
    everything = everything.reshape(cand_count * tile_count, block_rows, feature_dim)
    owners = jnp.arange(cand_count, dtype=jnp.int32)[:, None] * tile_count
    mirrors = jnp.take(everything, (owners + wanted).reshape(-1), axis=0)
    tile_values = adj_values[0, 0]
    block_count = tile_values.shape[0]
    stride = math.gcd(block_count, 16)
    turns = block_count // stride
    live_mask = (jnp.arange(block_count, dtype=jnp.int32) < live_blocks[0, 0]).astype(jnp.float32)
    packed = (
        tile_values.reshape(turns, stride, block_rows, block_rows),
        adj_source[0, 0].reshape(turns, stride),
        adj_target[0, 0].reshape(turns, stride),
        adj_relation[0, 0].reshape(turns, stride),
        live_mask.reshape(turns, stride),
    )

    def forward_turn(partial_value, inputs_now):
        values_now, source_now, target_now, relation_now, live_now = inputs_now
        composed = (
            jnp.take(mirrors, source_now, axis=0).astype(jnp.float32)
            - jnp.take(rel_emb, relation_now, axis=0)[:, None, :]
        ).astype(jnp.bfloat16)
        messages = jnp.einsum(
            "bij,bjd->bid", values_now, composed, preferred_element_type=jnp.float32
        )
        messages = messages * live_now[:, None, None]
        return (partial_value.at[target_now].add(messages), None)

    partial_value, ignored = lax.scan(
        forward_turn, jnp.zeros((tile_count, block_rows, feature_dim), jnp.float32), packed
    )
    aggregate = lax.psum_scatter(
        partial_value.reshape(node_rows, feature_dim), "grp", scatter_dimension=0, tiled=True
    )
    aggregate_bf = aggregate.astype(jnp.bfloat16)
    own_rows = lax.dynamic_slice_in_dim(nodes, grp_index * share_rows, share_rows, 0)
    pre_act = jnp.dot(aggregate_bf, w_in, preferred_element_type=jnp.float32) + jnp.dot(
        own_rows, w_self, preferred_element_type=jnp.float32
    )
    activated = jnp.tanh(pre_act)
    h_new = activated.astype(jnp.bfloat16)
    first_row = cand_index * node_rows + grp_index * share_rows
    row_ids = first_row + jnp.arange(share_rows, dtype=jnp.int32)
    head_pick = query_head[:, None] == row_ids[None, :]
    head_part = jnp.dot(head_pick.astype(jnp.bfloat16), h_new, preferred_element_type=jnp.float32)
    heads = lax.psum(head_part, ("grp", "cand"))
    queries = heads + jnp.take(rel_score, query_rel, axis=0)
    cand_rows = h_new.astype(jnp.float32)
    scale = feature_dim ** (-0.5)
    cross = jnp.dot(queries, cand_rows.T, precision=HIGH)
    scores = -scale * (
        jnp.sum(queries * queries, axis=1)[:, None]
        + jnp.sum(cand_rows * cand_rows, axis=1)[None, :]
        - 2.0 * cross
    )
    block_ids = first_row // block_rows + jnp.arange(share_rows // block_rows, dtype=jnp.int32)
    block_ok = jnp.any(allowed[:, :, None] == block_ids[None, None, :], axis=1)
    allowed_mask = jnp.repeat(block_ok, block_rows, axis=1)
    tail_pick = true_tail[:, None] == row_ids[None, :]
    truth_part = jnp.sum(jnp.where(tail_pick, scores, 0.0), axis=1)
    local_max = jnp.max(jnp.where(allowed_mask, scores, NEG_FILL), axis=1)
    row_max = lax.pmax(local_max, ("grp", "cand"))
    local_total = jnp.sum(
        jnp.exp(jnp.where(allowed_mask, scores - row_max[:, None], NEG_FILL)), axis=1
    )
    row_total, truth = lax.psum((local_total, truth_part), ("grp", "cand"))
    log_norm = row_max + jnp.log(row_total)
    loss = log_norm - truth
    prob = jnp.exp(jnp.where(allowed_mask, scores - log_norm[:, None], NEG_FILL))
    grad_score = (prob - tail_pick.astype(jnp.float32)) / query_head.shape[0]
    query_part = (
        2.0
        * scale
        * (
            jnp.dot(grad_score, cand_rows, precision=HIGH)
            - queries * jnp.sum(grad_score, axis=1)[:, None]
        )
    )
    query_grad = lax.psum(query_part, ("grp", "cand"))
    cand_grad = (
        2.0
        * scale
        * (
            jnp.dot(grad_score.T, queries, precision=HIGH)
            - cand_rows * jnp.sum(grad_score, axis=0)[:, None]
        )
    )
    row_grad = cand_grad + jnp.dot(head_pick.astype(jnp.float32).T, query_grad, precision=HIGH)
    pre_grad = (row_grad * (1.0 - activated * activated)).astype(jnp.bfloat16)
    grad_w_in, grad_w_self = lax.psum(
        (
            jnp.dot(aggregate_bf.T, pre_grad, preferred_element_type=jnp.float32),
            jnp.dot(own_rows.T, pre_grad, preferred_element_type=jnp.float32),
        ),
        ("grp", "cand"),
    )
    agg_grad = jnp.dot(pre_grad, w_in.T, preferred_element_type=jnp.float32).astype(jnp.bfloat16)
    agg_tiles = lax.all_gather(agg_grad, "grp", axis=0, tiled=True).reshape(
        tile_count, block_rows, feature_dim
    )

    def backward_turn(carry, inputs_now):
        mirror_grad, relation_grad = carry
        values_now, source_now, target_now, relation_now, live_now = inputs_now
        composed_grad = jnp.einsum(
            "bij,bid->bjd",
            values_now,
            jnp.take(agg_tiles, target_now, axis=0),
            preferred_element_type=jnp.float32,
        )
        composed_grad = composed_grad * live_now[:, None, None]
        mirror_grad = mirror_grad.at[source_now].add(composed_grad)
        relation_grad = relation_grad.at[relation_now].add(-jnp.sum(composed_grad, axis=1))
        return ((mirror_grad, relation_grad), None)

    start = (
        jnp.zeros((mirror_count, block_rows, feature_dim), jnp.float32),
        jnp.zeros(rel_emb.shape, jnp.float32),
    )
    (mirror_grad, relation_grad), ignored = lax.scan(backward_turn, start, packed)
    grad_rel = lax.psum(relation_grad, "cand")
    returned = lax.all_to_all(
        mirror_grad.reshape(cand_count, slot_count, block_rows, feature_dim).astype(jnp.bfloat16),
        "cand",
        split_axis=0,
        concat_axis=0,
        tiled=True,
    ).astype(jnp.float32)
    owned = (
        jnp.zeros((tile_count, block_rows, feature_dim), jnp.float32)
        .at[requested.reshape(-1)]
        .add(returned.reshape(mirror_count, block_rows, feature_dim))
    )
    node_grad = lax.psum_scatter(
        owned.reshape(node_rows, feature_dim).astype(jnp.bfloat16),
        "grp",
        scatter_dimension=0,
        tiled=True,
    ).astype(jnp.float32)
    node_grad = node_grad + jnp.dot(pre_grad, w_self.T, preferred_element_type=jnp.float32)
    return (h_new[None], loss, node_grad[None], grad_rel, grad_w_in, grad_w_self)


def solution(mesh):
    return jax.shard_map(
        body,
        mesh=mesh,
        in_specs=(
            P("cand", None, None),
            P("grp", None),
            P(),
            P(),
            P(),
            P("grp", "cand", None, None),
            P("grp", "cand", None, None, None),
            P("grp", "cand", None),
            P("grp", "cand", None),
            P("grp", "cand", None),
            P("grp", "cand"),
            P(),
            P(),
            P(),
            P(),
        ),
        out_specs=(P("cand", "grp", None), P(), P("cand", "grp", None), P("grp", None), P(), P()),
        check_vma=False,
    )
```

profile of v0, /device:TPU:1, one launch (start us, length us, event | category | flops | bytes accessed | tf_op | source)
XLA Modules:
  0.0 1358.5 jit_solution(7435921861001893714)
XLA Ops:
  14.8 71.8 %all-gather.2.cloned.1.call-done = bf16[32,512,512]{2,1,0:T(8,128)(2,1)} async-done(((bf16[1,512,512]{2,1,0:T(8,128)(2,1)}), bf16[32,512,512]{2,1,0:T(8,128)(2,1)}) %all-gather.2.cloned.1.call-update) | async-done | bytes 16777232 | tf_op jit(solution)/shard_map/all_gather | solution.py:41
  86.6 8.5 gather_fusion.3
  95.1 4.6 broadcast_select_fusion.1
  99.8 187.6 %while.22 = (s32[]{:T(128)}, f32[4,128,512]{2,1,0:T(8,128)S(1)}, s32[12,16]{1,0:T(8,128)S(1)}, bf16[12,16,128,128]{3,2,1,0:T(8,128)(2,1)}, s32[12,16]{1,0:T(8,12...) while((s32[]{:T(128)}, f32[4,128,512]{2,1,0:T(8,128)S(1)}, ...), condition=%wide.region_2.3_spmd, body=%wide.region_0.0_spmd.sunk | while | flops 274737504 | bytes 23766708 | solution.py:70
  109.4 6.1 scatter_fusion
  120.4 4.6 convolution_multiply_fusion.4
  125.0 6.1 scatter_fusion
  140.6 6.1 scatter_fusion
  151.7 4.6 convolution_multiply_fusion.4
  156.3 6.1 scatter_fusion
  171.9 6.1 scatter_fusion
  187.5 6.1 scatter_fusion
  203.1 6.1 scatter_fusion
  218.8 6.1 scatter_fusion
  234.4 6.1 scatter_fusion
  250.0 6.1 scatter_fusion
  265.7 6.1 scatter_fusion
  281.3 6.1 scatter_fusion
  288.5 21.3 %reduce-scatter.3.cloned.1.call-done = f32[128,512]{1,0:T(8,128)} async-done(((f32[512,512]{1,0:T(8,128)}), f32[128,512]{1,0:T(8,128)}) %reduce-scatter.3.cloned.1.call-update) | async-done | bytes 262160 | tf_op jit(solution)/shard_map/reduce_scatter | solution.py:73
  314.4 4.9 gather_fusion.4
  319.4 147.5 %all-reduce.6.cloned.1.call-done = f32[1024,512]{1,0:T(8,128)} async-done(((f32[1024,512]{1,0:T(8,128)}), f32[1024,512]{1,0:T(8,128)}) %all-reduce.6.cloned.1.call-update) | async-done | bytes 2097168 | tf_op jit(solution)/shard_map/psum | solution.py:87
  472.4 63.8 %pmax.7 = f32[1024]{0:T(1024)S(1)} all-reduce(f32[1024]{0:T(1024)S(1)} %get-tuple-element.185), channel_id=1, replica_groups=mesh['grp'=4,'cand'=32] {'grp','cand'}, use_global_device_ids=true, to_apply=%region_9.10 | all-reduce | flops 1024 | bytes 8192 | tf_op jit(solution)/shard_map/pmax | solution.py:103
  536.3 63.8 %psum.50 = f32[1024]{0:T(1024)S(1)} all-reduce(f32[1024]{0:T(1024)S(1)} %exponential_reduce_fusion), channel_id=1, replica_groups=mesh['grp'=4,'cand'=32] {'grp','cand'}, use_global_device_ids=true, to_apply=%region_11.12 | all-reduce | flops 1024 | bytes 8192 | tf_op jit(solution)/shard_map/psum | solution.py:107
  605.9 4.7 all-to-all-start
  610.6 8.6 copy.26
  622.2 130.2 %all-reduce.8.cloned.1.call-done = f32[1024,512]{1,0:T(8,128)} async-done(((f32[1024,512]{1,0:T(8,128)}), f32[1024,512]{1,0:T(8,128)}) %all-reduce.8.cloned.1.call-update) | async-done | bytes 2097168 | tf_op jit(solution)/shard_map/psum | solution.py:120
  755.2 10.5 all_gather.7
  770.0 204.7 %while.23 = (s32[]{:T(128)}, f32[32,128,512]{2,1,0:T(8,128)}, f32[225,512]{1,0:T(8,128)S(1)}, s32[12,16]{1,0:T(8,128)S(1)}, bf16[12,16,128,128]{2,3,1,0:T(8,128)...) while((s32[]{:T(128)}, f32[32,128,512]{2,1,0:T(8,128)}, ...), condition=%wide.region_21.22_spmd, body=%wide.region_17.21_spmd.sunk | while | flops 272639232 | bytes 24124884 | solution.py:161
  776.6 9.7 scatter_fusion.1
  793.8 9.5 scatter_fusion.1
  810.7 9.6 scatter_fusion.1
  827.8 9.7 scatter_fusion.1
  845.0 9.6 scatter_fusion.1
  862.0 9.8 scatter_fusion.1
  879.3 9.5 scatter_fusion.1
  896.2 9.7 scatter_fusion.1
  913.3 9.6 scatter_fusion.1
  930.3 9.5 scatter_fusion.1
  947.3 9.6 scatter_fusion.1
  964.3 9.5 scatter_fusion.1
  974.7 6.1 convert_bitcast_fusion
  980.9 8.8 all-to-all-start.1
  990.4 51.4 %all-to-all-done.1 = bf16[32,1,128,512]{3,2,1,0:T(8,128)(2,1)} async-done(((bf16[32,1,128,512]{3,2,1,0:T(8,128)(2,1)}), bf16[32,1,128,512]{3,2,1,0:T(8,128)(2,1)}, u32[]{:S(2)}, u32[]{:S(2)}) %all-to-all-start.1) | async-done | bytes 4194336 | tf_op jit(solution)/shard_map/all_to_all | solution.py:163
  1041.8 6.6 bitcast_convert_fusion
  1048.4 11.7 scatter_fusion.2
  1065.2 65.0 %psum.51 = f32[1024]{0:T(1024)S(1)} all-reduce(f32[1024]{0:T(1024)S(1)} %get-tuple-element.133), channel_id=1, replica_groups=mesh['grp'=4,'cand'=32] {'grp','cand'}, use_global_device_ids=true, to_apply=%region_13.14 | all-reduce | flops 1024 | bytes 8192 | tf_op jit(solution)/shard_map/psum | solution.py:107
  1132.7 57.1 %all-reduce.10.cloned.1.call-done = f32[225,512]{1,0:T(8,128)} async-done(((f32[225,512]{1,0:T(8,128)}), f32[225,512]{1,0:T(8,128)}) %all-reduce.10.cloned.1.call-update) | async-done | bytes 460816 | tf_op jit(solution)/shard_map/psum | solution.py:162
  1189.8 156.6 %all-reduce.12.cloned.1.call-done = (f32[512,512]{1,0:T(8,128)}, f32[512,512]{1,0:T(8,128)}) async-done(((f32[512,512]{1,0:T(8,128)}, f32[512,512]{1,0:T(8,128)}), (f32[512,512]{1,0:T(8,128)}, f32[512,512]{1,0:T(8,128)})) %all-reduce.12.cloned.1.call-update) | async-done | bytes 2097168 | tf_op jit(solution)/shard_map/psum | solution.py:131
  (304 shorter events, 241.0 us)
Async XLA Ops:
  7.2 307.2 %copy-start = (f32[900,512]{1,0:T(8,128)S(1)}, f32[900,512]{1,0:T(8,128)}, u32[]{:S(2)}) copy-start(f32[900,512]{1,0:T(8,128)} %param.23) | copy-start | bytes 5529604
  7.2 79.4 %all-gather.2.cloned.1.call-start = ((), (), s32[]{:S(2)}) async-start(), calls=%async_computation.4 | async-start | bytes 17301504 | tf_op jit(solution)/shard_map/all_gather | solution.py:41
  7.9 301.9 %reduce-scatter.3.cloned.1.call-start = ((), (), s32[]{:S(2)}) async-start(), calls=%async_computation.5 | async-start | bytes 1310720 | tf_op jit(solution)/shard_map/reduce_scatter | solution.py:73
  95.1 4.8 copy-start.4
  287.4 1.0 copy-start.2
  287.4 23.7 %copy-start.7 = (bf16[512,512]{1,0:T(8,128)(2,1)S(1)}, bf16[512,512]{1,0:T(8,128)(2,1)}, u32[]{:S(2)}) copy-start(bf16[512,512]{1,0:T(8,128)(2,1)} %param.22) | copy-start | bytes 1572868
  287.4 25.0 %copy-start.13 = (s32[1024]{0:T(1024)S(1)}, s32[1024]{0:T(1024)}, u32[]{:S(2)}) copy-start(s32[1024]{0:T(1024)} %param.30) | copy-start | bytes 12292
  288.4 178.4 %all-reduce.6.cloned.1.call-start = ((), (), s32[]{:S(2)}) async-start(), calls=%async_computation.6 | async-start | bytes 4194304 | tf_op jit(solution)/shard_map/psum | solution.py:87
  312.4 306.8 %copy-start.5 = (bf16[128,512]{1,0:T(8,128)(2,1)}, bf16[128,512]{1,0:T(8,128)(2,1)S(1)}, u32[]{:S(2)}) copy-start(bf16[128,512]{1,0:T(8,128)(2,1)S(1)} %get-tuple-element.175) | copy-start | bytes 393220
  312.4 2.0 copy-start.14
  314.3 438.1 %all-reduce.8.cloned.1.call-start = ((), (), s32[]{:S(2)}) async-start(), calls=%async_computation.7 | async-start | bytes 4194304 | tf_op jit(solution)/shard_map/psum | solution.py:120
  314.4 4.9 copy-start.12
  469.7 1.3 copy-start.3
  469.7 130.3 %copy-start.11 = (s32[1024]{0:T(1024)S(1)}, s32[1024]{0:T(1024)}, u32[]{:S(2)}) copy-start(s32[1024]{0:T(1024)} %param.33) | copy-start | bytes 12292
  604.6 0.7 copy-start.15
  605.9 374.9 %all-to-all-start = ((s32[32,1,1]{2,1,0:T(1,128)}), s32[32,1,1]{2,1,0:T(1,128)S(1)}, u32[]{:S(2)}, u32[]{:S(2)}) async-start(s32[32,1,1]{2,1,0:T(1,128)} %copy.28), calls=%async_computation.1 | async-start | bytes 32768 | tf_op jit(solution)/shard_map/all_to_all | solution.py:40
  622.2 132.7 %copy-start.6 = (bf16[512,512]{1,0:T(8,128)(2,1)S(1)}, bf16[512,512]{1,0:T(8,128)(2,1)}, u32[]{:S(2)}) copy-start(bf16[512,512]{1,0:T(8,128)(2,1)} %param.21) | copy-start | bytes 1572868
  974.7 6.2 copy-start.8
  980.9 60.9 %all-to-all-start.1 = ((bf16[32,1,128,512]{3,2,1,0:T(8,128)(2,1)}), bf16[32,1,128,512]{3,2,1,0:T(8,128)(2,1)}, u32[]{:S(2)}, u32[]{:S(2)}) async-start(bf16[32,1,128,512]{3,2,1,0:T(8,128)(2,1)} %convert_bitcast_fusion), calls=%async_computation.2 | async-start | bytes 8388608 | tf_op jit(solution)/shard_map/all_to_all | solution.py:163
  989.7 141.1 %reduce-scatter.5.cloned.1.call-start = ((), (), s32[]{:S(2)}) async-start(), calls=%async_computation.8 | async-start | bytes 655360 | tf_op jit(solution)/shard_map/reduce_scatter | solution.py:175
  1060.1 1.5 copy-start.10
  1061.0 128.7 %all-reduce.10.cloned.1.call-start = ((), (), s32[]{:S(2)}) async-start(), calls=%async_computation.9 | async-start | bytes 950272 | tf_op jit(solution)/shard_map/psum | solution.py:162
  1061.6 284.8 %all-reduce.12.cloned.1.call-start = ((), (), s32[]{:S(2)}) async-start(), calls=%async_computation.10 | async-start | bytes 4194304 | tf_op jit(solution)/shard_map/psum | solution.py:131
  1346.4 4.2 copy-start.9
  1346.4 5.2 copy-start.1
Sparse Core Ops, SparseCore 0:
  10.3 76.2 all-gather.1
  288.5 21.2 reduce-scatter.2
  314.7 152.1 all-reduce.5
  604.7 147.6 all-reduce.7
  1061.2 19.2 reduce-scatter.4
  1084.1 105.5 all-reduce.9
  1195.4 150.9 all-reduce.11
where the time goes:
time: 1360 us
  waiting for transfers between devices  637 us (47%)
  other arithmetic  241 us (18%)
  blocking collectives  203 us (15%)
  matrix products  130 us (10%)
  local copies, waits for them, and re-layouts  117 us (9%)
  between operations  15.1 us (1%)
  starting transfers between devices  13.8 us (1%)
    psum x1, waiting for transfers between devices, body(): lax.psum((jnp.dot(aggregate_bf.T, pre_grad, preferred_element_type=jnp.fl...  157 us
    psum x1, waiting for transfers between devices, body(): heads = lax.psum(head_part, ('grp', 'cand'))  147 us
    psum x1, waiting for transfers between devices, body(): query_grad = lax.psum(query_part, ('grp', 'cand'))  130 us
    psum x2, blocking collectives, body(): row_total, truth = lax.psum((local_total, truth_part), ('grp', 'cand'))  129 us
    scatter-add x12, other arithmetic, backward_turn(): mirror_grad = mirror_grad.at[source_now].add(composed_grad)  115 us
    scatter-add x12, other arithmetic, forward_turn(): return (partial_value.at[target_now].add(messages), None)  73.3 us
    all_gather x1, waiting for transfers between devices, body(): everything = lax.all_gather(node_emb, 'cand', axis=0, tiled=True)  71.8 us
    pmax x1, blocking collectives, body(): row_max = lax.pmax(local_max, ('grp', 'cand'))  63.8 us
  transfers between devices with their start and end apart: 9, of which 7 were waited for; matrix products, arithmetic and copies ran while one was open for 18% of the time, Pallas kernels for 0%

commit v1 on v0

--- a/solution.py
+++ b/solution.py
@@ -6,6 +6,14 @@
 
 NEG_FILL = -1e30
 HIGH = lax.Precision.HIGHEST
+
+
+def added_up(value, axis):
+    devices, total = (lax.axis_size(axis), value)
+    for far in [1 << k for k in range(devices.bit_length() - 1)]:
+        route = [(i, i ^ far) for i in range(devices)]
+        total = total + lax.ppermute(total, axis, route)
+    return total
 
 
 def body(
@@ -159,7 +167,7 @@
         jnp.zeros(rel_emb.shape, jnp.float32),
     )
     (mirror_grad, relation_grad), ignored = lax.scan(backward_turn, start, packed)
-    grad_rel = lax.psum(relation_grad, "cand")
+    grad_rel = added_up(relation_grad, "cand")
     returned = lax.all_to_all(
         mirror_grad.reshape(cand_count, slot_count, block_rows, feature_dim).astype(jnp.bfloat16),
         "cand",

time: 1360 us -> 1250 us (0.919)
  waiting for transfers between devices: 637 us -> 520 us
    psum x1, waiting for transfers between devices: 157 us -> 78.7 us  [body(): lax.psum((jnp.dot(aggregate_bf.T, pre_grad, preferred_element_type=jnp.fl...]
    psum x1 -> x0, waiting for transfers between devices: 57.1 us -> none  [body(): grad_rel = lax.psum(relation_grad, 'cand')]
    ppermute x0 -> x5, waiting for transfers between devices: none -> 21 us  [added_up(): total = total + lax.ppermute(total, axis, route)]
  transfers between devices with their start and end apart: 9 -> 13, of which waited for: 7 -> 9; matrix products, arithmetic and copies ran while one was open for 18% -> 21% of each run, Pallas kernels for 0% -> 0%
where the time goes in v1:
time: 1250 us
  waiting for transfers between devices  520 us (42%)
  other arithmetic  241 us (19%)
  blocking collectives  206 us (16%)
  matrix products  130 us (10%)
  local copies, waits for them, and re-layouts  116 us (9%)
  starting transfers between devices  19 us (2%)
  between operations  15.1 us (1%)
    psum x1, waiting for transfers between devices, body(): heads = lax.psum(head_part, ('grp', 'cand'))  147 us
    psum x2, blocking collectives, body(): row_total, truth = lax.psum((local_total, truth_part), ('grp', 'cand'))  132 us
    psum x1, waiting for transfers between devices, body(): query_grad = lax.psum(query_part, ('grp', 'cand'))  130 us
    scatter-add x12, other arithmetic, backward_turn(): mirror_grad = mirror_grad.at[source_now].add(composed_grad)  115 us
    psum x1, waiting for transfers between devices, body(): lax.psum((jnp.dot(aggregate_bf.T, pre_grad, preferred_element_type=jnp.fl...  78.7 us
    scatter-add x12, other arithmetic, forward_turn(): return (partial_value.at[target_now].add(messages), None)  73.3 us
    all_gather x1, waiting for transfers between devices, body(): everything = lax.all_gather(node_emb, 'cand', axis=0, tiled=True)  71.8 us
    pmax x1, blocking collectives, body(): row_max = lax.pmax(local_max, ('grp', 'cand'))  63.8 us
  transfers between devices with their start and end apart: 13, of which 9 were waited for; matrix products, arithmetic and copies ran while one was open for 21% of the time, Pallas kernels for 0%

profile of v1, /device:TPU:1, one launch (start us, length us, event | category | flops | bytes accessed | tf_op | source)
XLA Modules:
  0.0 1248.6 jit_solution(9790075393450332530)
XLA Ops:
  14.8 71.8 %all-gather.2.cloned.1.call-done = bf16[32,512,512]{2,1,0:T(8,128)(2,1)} async-done(((bf16[1,512,512]{2,1,0:T(8,128)(2,1)}), bf16[32,512,512]{2,1,0:T(8,128)(2,1)}) %all-gather.2.cloned.1.call-update) | async-done | bytes 16777232 | tf_op jit(solution)/shard_map/all_gather | solution.py:49
  86.6 8.5 gather_fusion.3
  95.1 4.6 broadcast_select_fusion.1
  99.8 187.6 %while.22 = (s32[]{:T(128)}, f32[4,128,512]{2,1,0:T(8,128)S(1)}, s32[12,16]{1,0:T(8,128)S(1)}, bf16[12,16,128,128]{3,2,1,0:T(8,128)(2,1)}, s32[12,16]{1,0:T(8,12...) while((s32[]{:T(128)}, f32[4,128,512]{2,1,0:T(8,128)S(1)}, ...), condition=%wide.region_2.3_spmd, body=%wide.region_0.0_spmd.sunk | while | flops 274737504 | bytes 23766708 | solution.py:78
  109.4 6.1 scatter_fusion
  125.0 6.1 scatter_fusion
  140.6 6.1 scatter_fusion
  151.7 4.6 convolution_multiply_fusion.4
  156.3 6.1 scatter_fusion
  171.9 6.1 scatter_fusion
  187.5 6.1 scatter_fusion
  203.1 6.1 scatter_fusion
  218.8 6.1 scatter_fusion
  234.4 6.1 scatter_fusion
  250.0 6.1 scatter_fusion
  265.7 6.1 scatter_fusion
  281.3 6.1 scatter_fusion
  288.5 21.3 %reduce-scatter.3.cloned.1.call-done = f32[128,512]{1,0:T(8,128)} async-done(((f32[512,512]{1,0:T(8,128)}), f32[128,512]{1,0:T(8,128)}) %reduce-scatter.3.cloned.1.call-update) | async-done | bytes 262160 | tf_op jit(solution)/shard_map/reduce_scatter | solution.py:81
  314.4 4.9 gather_fusion.4
  319.4 147.5 %all-reduce.5.cloned.1.call-done = f32[1024,512]{1,0:T(8,128)} async-done(((f32[1024,512]{1,0:T(8,128)}), f32[1024,512]{1,0:T(8,128)}) %all-reduce.5.cloned.1.call-update) | async-done | bytes 2097168 | tf_op jit(solution)/shard_map/psum | solution.py:95
  472.4 63.8 %pmax.7 = f32[1024]{0:T(1024)S(1)} all-reduce(f32[1024]{0:T(1024)S(1)} %get-tuple-element.185), channel_id=1, replica_groups=mesh['grp'=4,'cand'=32] {'grp','cand'}, use_global_device_ids=true, to_apply=%region_9.10 | all-reduce | flops 1024 | bytes 8192 | tf_op jit(solution)/shard_map/pmax | solution.py:111
  536.3 63.8 %psum.43 = f32[1024]{0:T(1024)S(1)} all-reduce(f32[1024]{0:T(1024)S(1)} %exponential_reduce_fusion), channel_id=1, replica_groups=mesh['grp'=4,'cand'=32] {'grp','cand'}, use_global_device_ids=true, to_apply=%region_11.12 | all-reduce | flops 1024 | bytes 8192 | tf_op jit(solution)/shard_map/psum | solution.py:115
  605.9 4.7 all-to-all-start
  610.7 8.6 copy.26
  622.3 130.1 %all-reduce.7.cloned.1.call-done = f32[1024,512]{1,0:T(8,128)} async-done(((f32[1024,512]{1,0:T(8,128)}), f32[1024,512]{1,0:T(8,128)}) %all-reduce.7.cloned.1.call-update) | async-done | bytes 2097168 | tf_op jit(solution)/shard_map/psum | solution.py:128
  755.2 10.5 all_gather.7
  770.1 204.6 %while.23 = (s32[]{:T(128)}, f32[32,128,512]{2,1,0:T(8,128)}, f32[225,512]{1,0:T(8,128)S(1)}, s32[12,16]{1,0:T(8,128)S(1)}, bf16[12,16,128,128]{2,3,1,0:T(8,128)...) while((s32[]{:T(128)}, f32[32,128,512]{2,1,0:T(8,128)}, ...), condition=%wide.region_21.22_spmd, body=%wide.region_17.21_spmd.sunk | while | flops 272639232 | bytes 24124884 | solution.py:169
  776.6 9.7 scatter_fusion.1
  793.8 9.5 scatter_fusion.1
  810.7 9.6 scatter_fusion.1
  827.8 9.7 scatter_fusion.1
  845.0 9.6 scatter_fusion.1
  862.1 9.8 scatter_fusion.1
  879.3 9.5 scatter_fusion.1
  896.2 9.7 scatter_fusion.1
  913.3 9.6 scatter_fusion.1
  930.4 9.5 scatter_fusion.1
  947.3 9.6 scatter_fusion.1
  964.4 9.5 scatter_fusion.1
  974.7 6.0 convert_bitcast_fusion
  980.7 8.8 all-to-all-start.1
  993.0 48.6 %all-to-all-done.1 = bf16[32,1,128,512]{3,2,1,0:T(8,128)(2,1)} async-done(((bf16[32,1,128,512]{3,2,1,0:T(8,128)(2,1)}), bf16[32,1,128,512]{3,2,1,0:T(8,128)(2,1)}, u32[]{:S(2)}, u32[]{:S(2)}) %all-to-all-start.1) | async-done | bytes 4194336 | tf_op jit(solution)/shard_map/all_to_all | solution.py:171
  1041.6 6.6 bitcast_convert_fusion
  1048.3 11.7 scatter_fusion.2
  1062.8 11.6 collective-permute-done.2
  1077.0 8.5 collective-permute-done.3
  1088.2 68.1 %psum.44 = f32[1024]{0:T(1024)S(1)} all-reduce(f32[1024]{0:T(1024)S(1)} %get-tuple-element.133), channel_id=1, replica_groups=mesh['grp'=4,'cand'=32] {'grp','cand'}, use_global_device_ids=true, to_apply=%region_13.14 | all-reduce | flops 1024 | bytes 8192 | tf_op jit(solution)/shard_map/psum | solution.py:115
  1159.7 78.7 %all-reduce.9.cloned.1.call-done = (f32[512,512]{1,0:T(8,128)}, f32[512,512]{1,0:T(8,128)}) async-done(((f32[512,512]{1,0:T(8,128)}, f32[512,512]{1,0:T(8,128)}), (f32[512,512]{1,0:T(8,128)}, f32[512,512]{1,0:T(8,128)})) %all-reduce.9.cloned.1.call-update) | async-done | bytes 2097168 | tf_op jit(solution)/shard_map/psum | solution.py:139
  (313 shorter events, 250.4 us)
Async XLA Ops:
  7.2 307.2 %copy-start = (f32[900,512]{1,0:T(8,128)S(1)}, f32[900,512]{1,0:T(8,128)}, u32[]{:S(2)}) copy-start(f32[900,512]{1,0:T(8,128)} %param.23) | copy-start | bytes 5529604
  7.2 79.4 %all-gather.2.cloned.1.call-start = ((), (), s32[]{:S(2)}) async-start(), calls=%async_computation.4 | async-start | bytes 17301504 | tf_op jit(solution)/shard_map/all_gather | solution.py:49
  7.9 301.9 %reduce-scatter.3.cloned.1.call-start = ((), (), s32[]{:S(2)}) async-start(), calls=%async_computation.5 | async-start | bytes 1310720 | tf_op jit(solution)/shard_map/reduce_scatter | solution.py:81
  95.1 4.8 copy-start.4
  287.4 1.0 copy-start.2
  287.4 23.7 %copy-start.7 = (bf16[512,512]{1,0:T(8,128)(2,1)S(1)}, bf16[512,512]{1,0:T(8,128)(2,1)}, u32[]{:S(2)}) copy-start(bf16[512,512]{1,0:T(8,128)(2,1)} %param.22) | copy-start | bytes 1572868
  287.4 25.0 %copy-start.12 = (s32[1024]{0:T(1024)S(1)}, s32[1024]{0:T(1024)}, u32[]{:S(2)}) copy-start(s32[1024]{0:T(1024)} %param.30) | copy-start | bytes 12292
  288.4 178.4 %all-reduce.5.cloned.1.call-start = ((), (), s32[]{:S(2)}) async-start(), calls=%async_computation.6 | async-start | bytes 4194304 | tf_op jit(solution)/shard_map/psum | solution.py:95
  312.4 306.8 %copy-start.5 = (bf16[128,512]{1,0:T(8,128)(2,1)}, bf16[128,512]{1,0:T(8,128)(2,1)S(1)}, u32[]{:S(2)}) copy-start(bf16[128,512]{1,0:T(8,128)(2,1)S(1)} %get-tuple-element.175) | copy-start | bytes 393220
  312.4 2.0 copy-start.13
  314.3 438.1 %all-reduce.7.cloned.1.call-start = ((), (), s32[]{:S(2)}) async-start(), calls=%async_computation.7 | async-start | bytes 4194304 | tf_op jit(solution)/shard_map/psum | solution.py:128
  314.4 4.9 copy-start.11
  469.7 1.3 copy-start.3
  469.7 130.4 %copy-start.10 = (s32[1024]{0:T(1024)S(1)}, s32[1024]{0:T(1024)}, u32[]{:S(2)}) copy-start(s32[1024]{0:T(1024)} %param.33) | copy-start | bytes 12292
  604.6 0.7 copy-start.14
  605.9 374.8 %all-to-all-start = ((s32[32,1,1]{2,1,0:T(1,128)}), s32[32,1,1]{2,1,0:T(1,128)S(1)}, u32[]{:S(2)}, u32[]{:S(2)}) async-start(s32[32,1,1]{2,1,0:T(1,128)} %copy.28), calls=%async_computation.1 | async-start | bytes 32768 | tf_op jit(solution)/shard_map/all_to_all | solution.py:48
  622.3 132.6 %copy-start.6 = (bf16[512,512]{1,0:T(8,128)(2,1)S(1)}, bf16[512,512]{1,0:T(8,128)(2,1)}, u32[]{:S(2)}) copy-start(bf16[512,512]{1,0:T(8,128)(2,1)} %param.21) | copy-start | bytes 1572868
  980.7 60.9 %all-to-all-start.1 = ((bf16[32,1,128,512]{3,2,1,0:T(8,128)(2,1)}), bf16[32,1,128,512]{3,2,1,0:T(8,128)(2,1)}, u32[]{:S(2)}, u32[]{:S(2)}) async-start(bf16[32,1,128,512]{3,2,1,0:T(8,128)(2,1)} %convert_bitcast_fusion), calls=%async_computation.2 | async-start | bytes 8388608 | tf_op jit(solution)/shard_map/all_to_all | solution.py:171
  989.5 168.3 %reduce-scatter.5.cloned.1.call-start = ((), (), s32[]{:S(2)}) async-start(), calls=%async_computation.8 | async-start | bytes 655360 | tf_op jit(solution)/shard_map/reduce_scatter | solution.py:183
  989.5 1.9 collective-permute-start
  991.5 69.4 %collective-permute-start.1 = (f32[225,512]{1,0:T(8,128)S(1)}, f32[225,512]{1,0:T(8,128)S(1)}, u32[]{:S(2)}, u32[]{:S(2)}) collective-permute-start(f32[225,512]{1,0:T(8,128)S(1)} %add.244), channel_id=1, source_target_pairs={{0,2},{1,3},{2,0},{3,1},{4,6},{5,7},{6,4},{7,5},{8,10},{9,11},{10,... | collective-permute-start | bytes 1382408 | tf_op jit(solution)/shard_map/ppermute | solution.py:15
  1060.0 1.5 copy-start.9
  1060.9 177.5 %all-reduce.9.cloned.1.call-start = ((), (), s32[]{:S(2)}) async-start(), calls=%async_computation.9 | async-start | bytes 4194304 | tf_op jit(solution)/shard_map/psum | solution.py:139
  1061.0 13.4 %collective-permute-start.2 = (f32[225,512]{1,0:T(8,128)S(1)}, f32[225,512]{1,0:T(8,128)S(1)}, u32[]{:S(2)}, u32[]{:S(2)}) collective-permute-start(f32[225,512]{1,0:T(8,128)S(1)} %add.245), channel_id=1, source_target_pairs={{0,4},{1,5},{2,6},{3,7},{4,0},{5,1},{6,2},{7,3},{8,12},{9,13},{10,... | collective-permute-start | bytes 1382408 | tf_op jit(solution)/shard_map/ppermute | solution.py:15
  1074.5 11.0 collective-permute-start.3
  1085.6 71.3 %collective-permute-start.4 = (f32[225,512]{1,0:T(8,128)S(1)}, f32[225,512]{1,0:T(8,128)S(1)}, u32[]{:S(2)}, u32[]{:S(2)}) collective-permute-start(f32[225,512]{1,0:T(8,128)S(1)} %add.247), channel_id=1, source_target_pairs={{0,16},{1,17},{2,18},{3,19},{4,20},{5,21},{6,22},{7,23},{8,24},{9,... | collective-permute-start | bytes 1382408 | tf_op jit(solution)/shard_map/ppermute | solution.py:15
  1238.4 2.4 copy-start.8
  1238.4 3.4 copy-start.1
Sparse Core Ops, SparseCore 0:
  10.3 76.2 all-gather.1
  288.5 21.2 reduce-scatter.2
  314.7 152.1 all-reduce.4
  604.7 147.6 all-reduce.6
  1061.0 18.4 reduce-scatter.4
  1084.9 153.3 all-reduce.8
